TPU v7x, 32 devices: a whole 2x2x4 slice. The times are simulated.
32 devices in a mesh: ia: 4 (over z), ja: 8 (over y, x, core).
Axes of the slice: x: 2, y: 2, z: 4, core: 2. Of those that a mesh axis runs over, the one named last changes fastest.
Arguments:
- pno_basis: bfloat16 [4, 16, 512, 128], P('ia', 'ja'), may hold values from -0.4375 to 0.4375
- domain_map: int32 [4, 16, 512], replicated, may hold values from 0 to 1023, as said below
- amplitudes: float32 [4, 16, 128, 128], P('ia', 'ja'), may hold values from -6 to 6
- exchange_ints: float32 [4, 16, 128, 128], P('ia', 'ja'), may hold values from -6 to 6
- pno_energy: float32 [4, 16, 128], P('ia', 'ja'), may hold values from 0.5 to 3
- row_energy: float32 [4], P('ia'), may hold values from -1.5 to -0.3
- column_energy: float32 [16], P('ja'), may hold values from -1.5 to -0.3
- coupling_rows: float32 [4, 4], P('ia'), may hold values from -0.6 to 0.6
- coupling_columns: float32 [16, 16], P(None, 'ja'), may hold values from -0.6 to 0.6
- row_neighbours: int32 [4, 16, 3], P('ia', 'ja'), may hold values from 0 to 3, as said below
- column_neighbours: int32 [4, 16, 15], P('ia', 'ja'), may hold values from 0 to 15, as said below
- row_counts: int32 [4, 16], P('ia', 'ja'), may hold values from 1 to 3
- column_counts: int32 [4, 16], P('ia', 'ja'), may hold values from 1 to 15
Outputs:
- new_amplitudes: float32 [4, 16, 128, 128], P('ia', 'ja')
- pair_energy: float32 [4, 16], P('ia', 'ja')
Inputs may be any that keep to these rules, and one draw needn't show every extreme that they name: `domain_map`: the 512 entries of one pair are distinct. `row_neighbours`: the 3 entries of a pair (i, j) are distinct and differ from i. `column_neighbours`: the 15 entries of a pair (i, j) are distinct and differ from j.
All inputs are finite; a program needn't handle non-finite values.
Results may differ from a plain program's by a relative error of at most 0.008.
Values may be sent and summed in bfloat16 or wider, within the bound.
A program may use at most 64 MiB of HBM per device.

v0:
```python
import jax
import jax.numpy as jnp
from jax import lax
from jax.sharding import PartitionSpec as P

ITERS = 2
level_shift = 0.3


def pair_intersections(packed):
    own_domain, own_basis, partner_domains, partner_bases = packed
    match = (own_domain[None, :, None] == partner_domains[:, None, :]).astype(jnp.bfloat16)
    picked = jnp.einsum(
        "suv,svb->sub", match, partner_bases, preferred_element_type=jnp.float32
    ).astype(jnp.bfloat16)
    return jnp.einsum("ua,sub->sab", own_basis, picked, preferred_element_type=jnp.float32).astype(
        jnp.bfloat16
    )


def local(
    pno_basis,
    domain_map,
    amplitudes,
    exchange_ints,
    pno_energy,
    row_energy,
    column_energy,
    coupling_rows,
    coupling_columns,
    row_neighbours,
    column_neighbours,
    row_counts,
    column_counts,
):
    pair_rows = pno_basis.shape[0]
    pair_columns = pno_basis.shape[1]
    domain_size = pno_basis.shape[2]
    width = amplitudes.shape[-1]
    total_rows = domain_map.shape[0]
    total_columns = domain_map.shape[1]
    own_pairs = pair_rows * pair_columns
    row_offset = lax.axis_index("ia") * pair_rows
    column_offset = lax.axis_index("ja") * pair_columns
    domain_rows = lax.dynamic_slice_in_dim(domain_map, row_offset, pair_rows, 0)
    domain_columns = lax.dynamic_slice_in_dim(domain_map, column_offset, pair_columns, 1)
    own_domain = lax.dynamic_slice_in_dim(domain_rows, column_offset, pair_columns, 1).reshape(
        own_pairs, domain_size
    )
    own_basis = pno_basis.reshape(own_pairs, domain_size, width)
    local_rows = jnp.arange(pair_rows, dtype=jnp.int32)[:, None, None]
    local_columns = jnp.arange(pair_columns, dtype=jnp.int32)[None, :, None]
    row_slots = (row_neighbours * pair_columns + local_columns).reshape(own_pairs, -1)
    column_slots = (local_rows * total_columns + column_neighbours).reshape(own_pairs, -1)
    row_live = (
        jnp.arange(row_neighbours.shape[2], dtype=jnp.int32)[None, None, :] < row_counts[:, :, None]
    )
    row_table = jnp.broadcast_to(coupling_rows[:, None, :], (pair_rows, pair_columns, total_rows))
    row_weight = jnp.where(row_live, jnp.take_along_axis(row_table, row_neighbours, axis=2), 0.0)
    column_live = (
        jnp.arange(column_neighbours.shape[2], dtype=jnp.int32)[None, None, :]
        < column_counts[:, :, None]
    )
    column_table = coupling_columns.T[None, :, :]
    column_weight = jnp.where(
        column_live, jnp.take_along_axis(column_table, column_neighbours, axis=2), 0.0
    )
    weights = jnp.concatenate(
        [row_weight.reshape(own_pairs, -1), column_weight.reshape(own_pairs, -1)], axis=1
    )
    partner_domains = jnp.concatenate(
        [
            domain_columns.reshape(total_rows * pair_columns, domain_size)[row_slots],
            domain_rows.reshape(pair_rows * total_columns, domain_size)[column_slots],
        ],
        axis=1,
    )

    def slot_pick(column_slab, row_slab):
        column_flat = column_slab.reshape(
            (column_slab.shape[0] * column_slab.shape[1],) + column_slab.shape[2:]
        )
        row_flat = row_slab.reshape((row_slab.shape[0] * row_slab.shape[1],) + row_slab.shape[2:])
        return jnp.concatenate([column_flat[row_slots], row_flat[column_slots]], axis=1)

    energy_gap = (
        pno_energy[:, :, :, None]
        + pno_energy[:, :, None, :]
        - row_energy[:, None, None, None]
        - column_energy[None, :, None, None]
    )
    current = amplitudes
    for iteration in range(ITERS):
        rounded = current.astype(jnp.bfloat16)
        column_bases, column_rounded = (
            lax.all_gather(pno_basis, "ia", axis=0, tiled=True),
            lax.all_gather(rounded, "ia", axis=0, tiled=True),
        )
        row_bases, row_rounded = (
            lax.all_gather(pno_basis, "ja", axis=1, tiled=True),
            lax.all_gather(rounded, "ja", axis=1, tiled=True),
        )
        partner_bases = slot_pick(column_bases, row_bases)
        intersections = lax.map(
            pair_intersections, (own_domain, own_basis, partner_domains, partner_bases)
        )
        intersection_wide = intersections.astype(jnp.float32)
        halved = jnp.einsum(
            "psab,psbc->psac",
            intersection_wide,
            slot_pick(column_rounded, row_rounded).astype(jnp.float32),
        ).astype(jnp.bfloat16)
        projected = jnp.einsum("psac,psdc->psad", halved.astype(jnp.float32), intersection_wide)
        coupled = jnp.sum(weights[:, :, None, None] * projected, axis=1).reshape(
            pair_rows, pair_columns, width, width
        )
        residual = exchange_ints + energy_gap * current - coupled
        current = current - residual / (energy_gap + level_shift)
    pair_energy = jnp.sum(
        exchange_ints * (2.0 * current - jnp.swapaxes(current, 2, 3)), axis=(2, 3)
    )
    return (current, pair_energy)


def solution(mesh):
    in_specs = (
        P("ia", "ja", None, None),
        P(),
        P("ia", "ja", None, None),
        P("ia", "ja", None, None),
        P("ia", "ja", None),
        P("ia"),
        P("ja"),
        P("ia", None),
        P(None, "ja"),
        P("ia", "ja", None),
        P("ia", "ja", None),
        P("ia", "ja"),
        P("ia", "ja"),
    )
    out_specs = (P("ia", "ja", None, None), P("ia", "ja"))
    return jax.shard_map(local, mesh=mesh, in_specs=in_specs, out_specs=out_specs, check_vma=False)
```

profile of v0, /device:TPU:0, one launch (start us, length us, event | category | flops | bytes accessed | tf_op | source)
XLA Modules:
  0.0 133.0 jit_solution(14398114743911281365)
XLA Ops:
  7.2 0.0 copy-start
  7.2 0.0 all-gather.3.cloned.1.call-start
  7.2 0.7 all-gather.3.cloned.1.call-update
  7.9 0.0 all-gather.5.cloned.1.call-start
  8.0 0.7 all-gather.5.cloned.1.call-update
  8.7 0.7 bitcast_or_fusion
  9.4 0.1 reshape.292
  9.5 0.6 gather_fusion.1
  10.2 0.1 reshape.284
  10.3 0.6 gather_fusion
  10.9 0.0 copy-done.2
  10.9 11.3 %all_gather.23 = bf16[1,16,128,128]{3,2,0,1:T(8,128)(2,1)S(1)} all-gather(bf16[1,2,128,128]{3,2,0,1:T(8,128)(2,1)S(1)} %convert_bitcast_fusion), channel_id=1, replica_groups=mesh['ia'=4,'ja'=8] {'ja'}, dimensions={1}, use_global_device_ids=true | all-gather | bytes 589824 | tf_op jit(solution)/shard_map/all_gather | solution.py:101
  22.3 0.7 gather_fusion.5
  23.0 0.0 copy-start.1
  23.0 16.9 %all_gather.22 = bf16[4,2,128,128]{3,2,1,0:T(8,128)(2,1)S(1)} all-gather(bf16[1,2,128,128]{3,2,1,0:T(8,128)(2,1)S(1)} %convert_element_type.21), channel_id=1, replica_groups=mesh['ia'=4,'ja'=8] {'ia'}, dimensions={0}, use_global_device_ids=true | all-gather | bytes 327680 | tf_op jit(solution)/shard_map/all_gather | solution.py:97
  39.9 0.6 gather_fusion.4
  40.5 0.1 reshape.348
  40.6 0.0 copy-start.11
  40.6 0.7 gather_fusion.8
  41.3 0.1 reshape.347
  41.3 0.1 reshape.356
  41.4 0.9 gather_fusion.9
  42.3 0.1 reshape.355
  43.0 0.1 copy.32
  43.2 0.1 fusion.60
  43.2 0.0 copy-done.8
  43.2 0.1 fusion.61
  43.3 0.1 pad_maximum_fusion.1
  43.4 1.1 all-gather.3.cloned.1.call-done
  44.5 1.9 %gather_fusion.2 = bf16[6,512,128]{2,1,0:T(8,128)(2,1)S(1)} fusion(bf16[8,512,128]{2,1,0:T(8,128)(2,1)} %bitcast.122, s32[1024]{0:T(1024)S(1)} %pad_clamp_fusion.1), kind=kCustom, calls=%fused_computation.2 | custom fusion | bytes 1572888 | tf_op jit(solution)/shard_map/gather | solution.py:84
  46.5 27.1 %all-gather.5.cloned.1.call-done = bf16[1,16,512,128]{3,2,0,1:T(8,128)(2,1)} async-done(((bf16[1,2,512,128]{3,2,0,1:T(8,128)(2,1)}), bf16[1,16,512,128]{3,2,0,1:T(8,128)(2,1)}) %all-gather.5.cloned.1.call-update) | async-done | bytes 2097168 | tf_op jit(solution)/shard_map/all_gather | solution.py:100
  73.6 4.6 %gather_fusion.3 = bf16[30,512,128]{2,1,0:T(8,128)(2,1)} fusion(bf16[16,512,128]{2,1,0:T(8,128)(2,1)} %bitcast.111, s32[1024]{0:T(1024)S(1)} %pad_clamp_fusion), kind=kCustom, calls=%fused_computation.3 | custom fusion | bytes 7864440 | tf_op jit(solution)/shard_map/gather | solution.py:84
  78.2 4.7 %pad_maximum_fusion = bf16[2,18,512,128]{3,2,1,0:T(8,128)(2,1)} fusion(bf16[2,15,512,128]{3,2,1,0:T(8,128)(2,1)} %bitcast.110, bf16[2,3,512,128]{3,2,1,0:T(8,128)(2,1)S(1)} %bitcast.114), kind=kLoop, calls=%fused_computation.26 | loop fusion | flops 2359296 | bytes 9437184 | tf_op jit(solution)/shard_map/concatenate | solution.py:84
  82.9 11.8 %while.2 = (s32[]{:T(128)}, bf16[2,18,128,128]{2,3,1,0:T(8,128)(2,1)}, s32[2,512]{1,0:T(2,128)S(1)}, s32[2,18,512]{2,1,0:T(8,128)S(1)}, bf16[2,18,512,128]{3,2,1...) while((s32[]{:T(128)}, bf16[2,18,128,128]{2,3,1,0:T(8,128)(2,1)}, s32[2,512]{1,0:T(2,128)S(1)}, ...), condition=%wide.region_1.2_spmd, body=%wide.region_0.0_spmd.sunk | while | flops 1516142592 | bytes 3210837 | solution.py:104
  82.9 5.9 %fusion.81 = bf16[2,18,128,128]{2,3,1,0:T(8,128)(2,1)} fusion(bf16[2,18,128,128]{2,3,1,0:T(8,128)(2,1)} %get-tuple-element.110, s32[]{:T(128)} %get-tuple-element.109, bf16[2,18,512,128]{3,2,1,0:T(8,128)(2,1)} %get-tuple-element.120, s32[18,512]{1,0:T(8,128)S(1)} %dynamic-slice_bitcast_fusion.4, s32[512]{0:T(512)S(1)} %bitcast.125, ...), kind=kOutput, calls=%fused_computation.20.clone.1 | convolution fusion | flops 1516142592 | bytes 3132928 | tf_op jit(solution)/shard_map/while/body/eval_jaxpr/ua,sub->sab/dot_general | solution.py:16
  88.9 5.8 %fusion.81 = bf16[2,18,128,128]{2,3,1,0:T(8,128)(2,1)} fusion(bf16[2,18,128,128]{2,3,1,0:T(8,128)(2,1)} %get-tuple-element.110, s32[]{:T(128)} %get-tuple-element.109, bf16[2,18,512,128]{3,2,1,0:T(8,128)(2,1)} %get-tuple-element.120, s32[18,512]{1,0:T(8,128)S(1)} %dynamic-slice_bitcast_fusion.4, s32[512]{0:T(512)S(1)} %bitcast.125, ...), kind=kOutput, calls=%fused_computation.20.clone.1 | convolution fusion | flops 1516142592 | bytes 3132928 | tf_op jit(solution)/shard_map/while/body/eval_jaxpr/ua,sub->sab/dot_general | solution.py:16
  94.7 2.6 %multiply_reduce_fusion.1 = f32[2,128,128]{2,1,0:T(8,128)S(1)} fusion(bf16[2,18,128,128]{2,3,1,0:T(8,128)(2,1)} %get-tuple-element.40, bf16[2,15,128,128]{3,2,1,0:T(8,128)(2,1)S(1)} %bitcast.117, bf16[2,3,128,128]{3,2,1,0:T(8,128)(2,1)S(1)} %bitcast.123, f32[2,18]{1,0:T(2,128)S(1)} %pad_maximum_fusion.1), kind=kOutput, calls=%fused_computation.28 | convolution fusion | flops 304316416 | bytes 2490512 | tf_op jit(solution)/shard_map/psac,psdc->psad/dot_general | solution.py:113
  97.4 0.1 fusion.66
  97.5 13.9 %all_gather.24 = bf16[4,2,128,128]{3,2,1,0:T(8,128)(2,1)S(1)} all-gather(bf16[1,2,128,128]{3,2,1,0:T(8,128)(2,1)S(1)} %get-tuple-element.59), channel_id=1, replica_groups=mesh['ia'=4,'ja'=8] {'ia'}, dimensions={0}, use_global_device_ids=true | all-gather | bytes 327680 | tf_op jit(solution)/shard_map/all_gather | solution.py:97
  111.5 9.8 %all_gather.25 = bf16[1,16,128,128]{3,2,0,1:T(8,128)(2,1)S(1)} all-gather(bf16[1,2,128,128]{3,2,0,1:T(8,128)(2,1)S(1)} %bitcast.121), channel_id=1, replica_groups=mesh['ia'=4,'ja'=8] {'ja'}, dimensions={1}, use_global_device_ids=true | all-gather | bytes 589824 | tf_op jit(solution)/shard_map/all_gather | solution.py:101
  121.3 0.7 gather_fusion.7
  122.0 0.6 gather_fusion.6
  122.6 2.6 %multiply_reduce_fusion = f32[2,128,128]{2,1,0:T(8,128)S(1)} fusion(bf16[2,18,128,128]{2,3,1,0:T(8,128)(2,1)} %get-tuple-element.40, bf16[2,15,128,128]{3,2,1,0:T(8,128)(2,1)S(1)} %bitcast.118, bf16[2,3,128,128]{3,2,1,0:T(8,128)(2,1)S(1)} %bitcast.124, f32[2,18]{1,0:T(2,128)S(1)} %pad_maximum_fusion.1), kind=kOutput, calls=%fused_computation.27 | convolution fusion | flops 304316416 | bytes 2490512 | tf_op jit(solution)/shard_map/psac,psdc->psad/dot_general | solution.py:113
  125.2 0.1 fusion.56
  125.4 0.0 copy-start.3
  125.4 0.1 copy.31
  125.5 0.6 fusion.54
  126.2 0.0 copy-done.3
  (37 shorter events, 0.2 us)
Async XLA Ops:
  7.2 2.3 %copy-start = (s32[4,16,512]{2,1,0:T(8,128)S(1)}, s32[4,16,512]{2,1,0:T(8,128)}, u32[]{:S(2)}) copy-start(s32[4,16,512]{2,1,0:T(8,128)} %param.16) | copy-start | bytes 393220
  7.2 3.0 %copy-start.7 = (s32[1,2,3]{2,1,0:T(2,128)S(1)}, s32[1,2,3]{2,1,0:T(2,128)}, u32[]{:S(2)}) copy-start(s32[1,2,3]{2,1,0:T(2,128)} %param.24) | copy-start | bytes 76
  7.2 3.7 %copy-start.2 = (f32[1,2,128,128]{3,2,1,0:T(8,128)S(1)}, f32[1,2,128,128]{3,2,1,0:T(8,128)}, u32[]{:S(2)}) copy-start(f32[1,2,128,128]{3,2,1,0:T(8,128)} %param.17) | copy-start | bytes 393220
  7.2 37.3 %all-gather.3.cloned.1.call-start = ((), (), s32[]{:S(2)}) async-start(), calls=%async_computation | async-start | bytes 1310720 | tf_op jit(solution)/shard_map/all_gather | solution.py:96
  7.9 65.7 %all-gather.5.cloned.1.call-start = ((), (), s32[]{:S(2)}) async-start(), calls=%async_computation.1 | async-start | bytes 2359296 | tf_op jit(solution)/shard_map/all_gather | solution.py:100
  22.3 18.3 %copy-start.12 = (f32[1,4]{1,0:T(1,128)S(1)}, f32[1,4]{1,0:T(1,128)}, u32[]{:S(2)}) copy-start(f32[1,4]{1,0:T(1,128)} %param.22) | copy-start | bytes 52
  23.0 18.4 %copy-start.1 = (f32[16,2]{0,1:T(2,128)S(1)}, f32[16,2]{0,1:T(2,128)}, u32[]{:S(2)}) copy-start(f32[16,2]{0,1:T(2,128)} %param.23) | copy-start | bytes 388
  39.9 3.1 %copy-start.4 = (f32[1,2,128,128]{3,2,1,0:T(8,128)S(1)}, f32[1,2,128,128]{3,2,1,0:T(8,128)}, u32[]{:S(2)}) copy-start(f32[1,2,128,128]{3,2,1,0:T(8,128)} %param.18) | copy-start | bytes 393220
  40.6 2.6 %copy-start.10 = (s32[1,2]{1,0:T(1,128)S(1)}, s32[1,2]{1,0:T(1,128)}, u32[]{:S(2)}) copy-start(s32[1,2]{1,0:T(1,128)} %param.26) | copy-start | bytes 28
  40.6 2.7 %copy-start.8 = (s32[1,2,15]{2,1,0:T(2,128)S(1)}, s32[1,2,15]{2,1,0:T(2,128)}, u32[]{:S(2)}) copy-start(s32[1,2,15]{2,1,0:T(2,128)} %param.25) | copy-start | bytes 364
  40.6 2.6 %copy-start.11 = (s32[1,2]{1,0:T(1,128)S(1)}, s32[1,2]{1,0:T(1,128)}, u32[]{:S(2)}) copy-start(s32[1,2]{1,0:T(1,128)} %param.27) | copy-start | bytes 28
  78.2 4.7 %copy-start.5 = (bf16[1,2,512,128]{3,2,1,0:T(8,128)(2,1)S(1)}, bf16[1,2,512,128]{3,2,1,0:T(8,128)(2,1)}, u32[]{:S(2)}) copy-start(bf16[1,2,512,128]{3,2,1,0:T(8,128)(2,1)} %param.15) | copy-start | bytes 786436
  94.7 2.7 %copy-start.6 = (f32[1,2,128]{2,1,0:T(2,128)S(1)}, f32[1,2,128]{2,1,0:T(2,128)}, u32[]{:S(2)}) copy-start(f32[1,2,128]{2,1,0:T(2,128)} %param.19) | copy-start | bytes 3076
  94.7 2.7 %copy-start.9 = (f32[2]{0:T(128)S(1)}, f32[2]{0:T(128)}, u32[]{:S(2)}) copy-start(f32[2]{0:T(128)} %param.21) | copy-start | bytes 28
  125.4 0.8 copy-start.3
Sparse Core Ops, SparseCore 0:
  9.6 34.9 all-gather.2
  46.4 27.1 all-gather.4
where the time goes:
time: 133 us
  blocking collectives  51.9 us (39%)
  waiting for transfers between devices  29.6 us (22%)
  matrix products  17 us (13%)
  between operations  15 us (11%)
  local copies, waits for them, and re-layouts  12.7 us (10%)
  other arithmetic  6.59 us (5%)
    all_gather x2, blocking collectives, local(): lax.all_gather(rounded, 'ia', axis=0, tiled=True)  30.8 us
    all_gather x1, waiting for transfers between devices, local(): lax.all_gather(pno_basis, 'ja', axis=1, tiled=True)  27.1 us
    all_gather x2, blocking collectives, local(): lax.all_gather(rounded, 'ja', axis=1, tiled=True)  21.1 us
    dot_general x2, matrix products, pair_intersections(): jnp.einsum('ua,sub->sab', own_basis, picked, preferred_element_type=jnp.f...  11.8 us
    gather x3, local copies, waits for them, and re-layouts, slot_pick(): row_flat[column_slots]  6.08 us
    dot_general x2, matrix products, local(): jnp.einsum('psac,psdc->psad', halved.astype(jnp.float32), intersection_wide)  5.29 us
    concatenate x1, other arithmetic, slot_pick(): jnp.concatenate([column_flat[row_slots], row_flat[column_slots]], axis=1)  4.69 us
    gather x3, local copies, waits for them, and re-layouts, slot_pick(): column_flat[row_slots]  3.09 us
  transfers between devices with their start and end apart: 2, of which 2 were waited for; matrix products, arithmetic and copies ran while one was open for 6% of the time, Pallas kernels for 0%

commit v1 on v0

--- a/solution.py
+++ b/solution.py
@@ -96,9 +96,15 @@
             lax.all_gather(pno_basis, "ia", axis=0, tiled=True),
             lax.all_gather(rounded, "ia", axis=0, tiled=True),
         )
+
+        def divide_forms_on(values, mesh_dim):
+            y_new = jax.lax.all_gather(values, mesh_dim)
+            w_next = jnp.concatenate(y_new, axis=1)
+            return w_next
+
         row_bases, row_rounded = (
             lax.all_gather(pno_basis, "ja", axis=1, tiled=True),
-            lax.all_gather(rounded, "ja", axis=1, tiled=True),
+            divide_forms_on(rounded, "ja"),
         )
         partner_bases = slot_pick(column_bases, row_bases)
         intersections = lax.map(

time: 133 us -> 133 us (level)
  no operation moved by 1% of the time
where the time goes in v1:
time: 133 us
  blocking collectives  52 us (39%)
  waiting for transfers between devices  29.7 us (22%)
  matrix products  17 us (13%)
  between operations  15 us (11%)
  local copies, waits for them, and re-layouts  12.7 us (10%)
  other arithmetic  6.56 us (5%)
    all_gather x2, blocking collectives, local(): lax.all_gather(rounded, 'ia', axis=0, tiled=True)  30.9 us
    all_gather x1, waiting for transfers between devices, local(): lax.all_gather(pno_basis, 'ja', axis=1, tiled=True)  27.1 us
    all_gather x2, blocking collectives, divide_forms_on(): y_new = jax.lax.all_gather(values, mesh_dim)  21.1 us
    dot_general x2, matrix products, pair_intersections(): jnp.einsum('ua,sub->sab', own_basis, picked, preferred_element_type=jnp.f...  11.8 us
    gather x3, local copies, waits for them, and re-layouts, slot_pick(): row_flat[column_slots]  6.08 us
    dot_general x2, matrix products, local(): jnp.einsum('psac,psdc->psad', halved.astype(jnp.float32), intersection_wide)  5.28 us
    concatenate x1, other arithmetic, slot_pick(): jnp.concatenate([column_flat[row_slots], row_flat[column_slots]], axis=1)  4.69 us
    gather x3, local copies, waits for them, and re-layouts, slot_pick(): column_flat[row_slots]  3.09 us
  transfers between devices with their start and end apart: 2, of which 2 were waited for; matrix products, arithmetic and copies ran while one was open for 6% of the time, Pallas kernels for 0%

profile of v1, /device:TPU:0, one launch (start us, length us, event | category | flops | bytes accessed | tf_op | source)
XLA Modules:
  0.0 133.1 jit_solution(12470380145079233270)
XLA Ops:
  7.2 0.0 copy-start
  7.2 0.0 all-gather.5.cloned.1.call-start
  7.2 0.7 all-gather.5.cloned.1.call-update
  7.9 0.0 all-gather.7.cloned.1.call-start
  8.0 0.7 all-gather.7.cloned.1.call-update
  8.7 0.7 bitcast_or_fusion
  9.4 0.1 reshape.284
  9.5 0.6 gather_fusion.1
  10.2 0.1 reshape.276
  10.3 0.6 gather_fusion
  10.9 0.0 copy-done.5
  10.9 11.3 %all-gather = bf16[8,2,128,128]{3,2,1,0:T(8,128)(2,1)S(1)} all-gather(bf16[1,2,128,128]{3,2,1,0:T(8,128)(2,1)S(1)} %convert_element_type.21), channel_id=2, replica_groups=mesh['ia'=4,'ja'=8] {'ja'}, dimensions={0}, use_global_device_ids=true | all-gather | bytes 589824 | tf_op jit(solution)/shard_map/all_gather | solution.py:101
  22.2 0.7 gather_fusion.5
  23.0 0.0 copy-start.1
  23.0 16.9 %all_gather.28 = bf16[4,2,128,128]{3,2,1,0:T(8,128)(2,1)S(1)} all-gather(bf16[1,2,128,128]{3,2,1,0:T(8,128)(2,1)S(1)} %convert_element_type.21), channel_id=1, replica_groups=mesh['ia'=4,'ja'=8] {'ia'}, dimensions={0}, use_global_device_ids=true | all-gather | bytes 327680 | tf_op jit(solution)/shard_map/all_gather | solution.py:97
  39.9 0.6 gather_fusion.4
  40.5 0.1 reshape.340
  40.6 0.0 copy-start.11
  40.6 0.7 gather_fusion.8
  41.2 0.1 reshape.339
  41.3 0.1 reshape.348
  41.4 0.0 copy-done.1
  41.4 0.9 gather_fusion.9
  42.3 0.1 reshape.347
  43.0 0.0 copy-done.3
  43.0 0.1 copy.30
  43.1 0.1 fusion.60
  43.2 0.1 fusion.61
  43.3 0.1 pad_maximum_fusion.1
  43.4 1.1 all-gather.5.cloned.1.call-done
  44.5 1.9 %gather_fusion.2 = bf16[6,512,128]{2,1,0:T(8,128)(2,1)S(1)} fusion(bf16[8,512,128]{2,1,0:T(8,128)(2,1)} %bitcast.118, s32[1024]{0:T(1024)S(1)} %pad_clamp_fusion.1), kind=kCustom, calls=%fused_computation.2 | custom fusion | bytes 1572888 | tf_op jit(solution)/shard_map/gather | solution.py:84
  46.5 27.1 %all-gather.7.cloned.1.call-done = bf16[1,16,512,128]{3,2,0,1:T(8,128)(2,1)} async-done(((bf16[1,2,512,128]{3,2,0,1:T(8,128)(2,1)}), bf16[1,16,512,128]{3,2,0,1:T(8,128)(2,1)}) %all-gather.7.cloned.1.call-update) | async-done | bytes 2097168 | tf_op jit(solution)/shard_map/all_gather | solution.py:106
  73.6 4.6 %gather_fusion.3 = bf16[30,512,128]{2,1,0:T(8,128)(2,1)} fusion(bf16[16,512,128]{2,1,0:T(8,128)(2,1)} %bitcast.108, s32[1024]{0:T(1024)S(1)} %pad_clamp_fusion), kind=kCustom, calls=%fused_computation.3 | custom fusion | bytes 7864440 | tf_op jit(solution)/shard_map/gather | solution.py:84
  78.2 4.7 %pad_maximum_fusion = bf16[2,18,512,128]{3,2,1,0:T(8,128)(2,1)} fusion(bf16[2,15,512,128]{3,2,1,0:T(8,128)(2,1)} %bitcast.107, bf16[2,3,512,128]{3,2,1,0:T(8,128)(2,1)S(1)} %bitcast.111), kind=kLoop, calls=%fused_computation.26 | loop fusion | flops 2359296 | bytes 9437184 | tf_op jit(solution)/shard_map/concatenate | solution.py:84
  82.9 11.8 %while.2 = (s32[]{:T(128)}, bf16[2,18,128,128]{2,3,1,0:T(8,128)(2,1)}, s32[2,512]{1,0:T(2,128)S(1)}, s32[2,18,512]{2,1,0:T(8,128)S(1)}, bf16[2,18,512,128]{3,2,1...) while((s32[]{:T(128)}, bf16[2,18,128,128]{2,3,1,0:T(8,128)(2,1)}, s32[2,512]{1,0:T(2,128)S(1)}, ...), condition=%wide.region_1.2_spmd, body=%wide.region_0.0_spmd.sunk | while | flops 1516142592 | bytes 3210837 | solution.py:110
  82.9 5.9 %fusion.81 = bf16[2,18,128,128]{2,3,1,0:T(8,128)(2,1)} fusion(bf16[2,18,128,128]{2,3,1,0:T(8,128)(2,1)} %get-tuple-element.110, s32[]{:T(128)} %get-tuple-element.109, bf16[2,18,512,128]{3,2,1,0:T(8,128)(2,1)} %get-tuple-element.120, s32[18,512]{1,0:T(8,128)S(1)} %dynamic-slice_bitcast_fusion.4, s32[512]{0:T(512)S(1)} %bitcast.121, ...), kind=kOutput, calls=%fused_computation.20.clone.1 | convolution fusion | flops 1516142592 | bytes 3132928 | tf_op jit(solution)/shard_map/while/body/eval_jaxpr/ua,sub->sab/dot_general | solution.py:16
  88.9 5.8 %fusion.81 = bf16[2,18,128,128]{2,3,1,0:T(8,128)(2,1)} fusion(bf16[2,18,128,128]{2,3,1,0:T(8,128)(2,1)} %get-tuple-element.110, s32[]{:T(128)} %get-tuple-element.109, bf16[2,18,512,128]{3,2,1,0:T(8,128)(2,1)} %get-tuple-element.120, s32[18,512]{1,0:T(8,128)S(1)} %dynamic-slice_bitcast_fusion.4, s32[512]{0:T(512)S(1)} %bitcast.121, ...), kind=kOutput, calls=%fused_computation.20.clone.1 | convolution fusion | flops 1516142592 | bytes 3132928 | tf_op jit(solution)/shard_map/while/body/eval_jaxpr/ua,sub->sab/dot_general | solution.py:16
  94.7 2.6 %multiply_reduce_fusion.1 = f32[2,128,128]{2,1,0:T(8,128)S(1)} fusion(bf16[2,18,128,128]{2,3,1,0:T(8,128)(2,1)} %get-tuple-element.40, bf16[2,15,128,128]{3,2,1,0:T(8,128)(2,1)S(1)} %bitcast.114, bf16[2,3,128,128]{3,2,1,0:T(8,128)(2,1)S(1)} %bitcast.119, f32[2,18]{1,0:T(2,128)S(1)} %pad_maximum_fusion.1), kind=kOutput, calls=%fused_computation.28 | convolution fusion | flops 304316416 | bytes 2490512 | tf_op jit(solution)/shard_map/psac,psdc->psad/dot_general | solution.py:119
  97.4 0.1 fusion.66
  97.5 9.8 %all-gather.1 = bf16[8,2,128,128]{3,2,1,0:T(8,128)(2,1)S(1)} all-gather(bf16[1,2,128,128]{3,2,1,0:T(8,128)(2,1)S(1)} %get-tuple-element.59), channel_id=3, replica_groups=mesh['ia'=4,'ja'=8] {'ja'}, dimensions={0}, use_global_device_ids=true | all-gather | bytes 589824 | tf_op jit(solution)/shard_map/all_gather | solution.py:101
  107.3 14.0 %all_gather.31 = bf16[4,2,128,128]{3,2,1,0:T(8,128)(2,1)S(1)} all-gather(bf16[1,2,128,128]{3,2,1,0:T(8,128)(2,1)S(1)} %get-tuple-element.59), channel_id=1, replica_groups=mesh['ia'=4,'ja'=8] {'ia'}, dimensions={0}, use_global_device_ids=true | all-gather | bytes 327680 | tf_op jit(solution)/shard_map/all_gather | solution.py:97
  121.3 0.7 gather_fusion.7
  122.1 0.6 gather_fusion.6
  122.7 2.6 %multiply_reduce_fusion = f32[2,128,128]{2,1,0:T(8,128)S(1)} fusion(bf16[2,18,128,128]{2,3,1,0:T(8,128)(2,1)} %get-tuple-element.40, bf16[2,15,128,128]{3,2,1,0:T(8,128)(2,1)S(1)} %bitcast.115, bf16[2,3,128,128]{3,2,1,0:T(8,128)(2,1)S(1)} %bitcast.120, f32[2,18]{1,0:T(2,128)S(1)} %pad_maximum_fusion.1), kind=kOutput, calls=%fused_computation.27 | convolution fusion | flops 304316416 | bytes 2490512 | tf_op jit(solution)/shard_map/psac,psdc->psad/dot_general | solution.py:119
  125.3 0.1 fusion.56
  125.5 0.0 copy-start.2
  125.5 0.1 copy.29
  125.6 0.6 fusion.54
  (36 shorter events, 0.2 us)
Async XLA Ops:
  7.2 2.3 %copy-start = (s32[4,16,512]{2,1,0:T(8,128)S(1)}, s32[4,16,512]{2,1,0:T(8,128)}, u32[]{:S(2)}) copy-start(s32[4,16,512]{2,1,0:T(8,128)} %param.16) | copy-start | bytes 393220
  7.2 3.0 %copy-start.7 = (s32[1,2,3]{2,1,0:T(2,128)S(1)}, s32[1,2,3]{2,1,0:T(2,128)}, u32[]{:S(2)}) copy-start(s32[1,2,3]{2,1,0:T(2,128)} %param.24) | copy-start | bytes 76
  7.2 3.7 %copy-start.5 = (f32[1,2,128,128]{3,2,1,0:T(8,128)S(1)}, f32[1,2,128,128]{3,2,1,0:T(8,128)}, u32[]{:S(2)}) copy-start(f32[1,2,128,128]{3,2,1,0:T(8,128)} %param.17) | copy-start | bytes 393220
  7.2 37.3 %all-gather.5.cloned.1.call-start = ((), (), s32[]{:S(2)}) async-start(), calls=%async_computation | async-start | bytes 1310720 | tf_op jit(solution)/shard_map/all_gather | solution.py:96
  7.9 65.7 %all-gather.7.cloned.1.call-start = ((), (), s32[]{:S(2)}) async-start(), calls=%async_computation.1 | async-start | bytes 2359296 | tf_op jit(solution)/shard_map/all_gather | solution.py:106
  22.2 18.3 %copy-start.12 = (f32[1,4]{1,0:T(1,128)S(1)}, f32[1,4]{1,0:T(1,128)}, u32[]{:S(2)}) copy-start(f32[1,4]{1,0:T(1,128)} %param.22) | copy-start | bytes 52
  23.0 18.4 %copy-start.1 = (f32[16,2]{0,1:T(2,128)S(1)}, f32[16,2]{0,1:T(2,128)}, u32[]{:S(2)}) copy-start(f32[16,2]{0,1:T(2,128)} %param.23) | copy-start | bytes 388
  39.9 3.1 %copy-start.3 = (f32[1,2,128,128]{3,2,1,0:T(8,128)S(1)}, f32[1,2,128,128]{3,2,1,0:T(8,128)}, u32[]{:S(2)}) copy-start(f32[1,2,128,128]{3,2,1,0:T(8,128)} %param.18) | copy-start | bytes 393220
  40.5 2.6 %copy-start.10 = (s32[1,2]{1,0:T(1,128)S(1)}, s32[1,2]{1,0:T(1,128)}, u32[]{:S(2)}) copy-start(s32[1,2]{1,0:T(1,128)} %param.26) | copy-start | bytes 28
  40.6 2.7 %copy-start.8 = (s32[1,2,15]{2,1,0:T(2,128)S(1)}, s32[1,2,15]{2,1,0:T(2,128)}, u32[]{:S(2)}) copy-start(s32[1,2,15]{2,1,0:T(2,128)} %param.25) | copy-start | bytes 364
  40.6 2.6 %copy-start.11 = (s32[1,2]{1,0:T(1,128)S(1)}, s32[1,2]{1,0:T(1,128)}, u32[]{:S(2)}) copy-start(s32[1,2]{1,0:T(1,128)} %param.27) | copy-start | bytes 28
  78.2 4.7 %copy-start.4 = (bf16[1,2,512,128]{3,2,1,0:T(8,128)(2,1)S(1)}, bf16[1,2,512,128]{3,2,1,0:T(8,128)(2,1)}, u32[]{:S(2)}) copy-start(bf16[1,2,512,128]{3,2,1,0:T(8,128)(2,1)} %param.15) | copy-start | bytes 786436
  94.7 2.7 %copy-start.6 = (f32[1,2,128]{2,1,0:T(2,128)S(1)}, f32[1,2,128]{2,1,0:T(2,128)}, u32[]{:S(2)}) copy-start(f32[1,2,128]{2,1,0:T(2,128)} %param.19) | copy-start | bytes 3076
  94.7 2.7 %copy-start.9 = (f32[2]{0:T(128)S(1)}, f32[2]{0:T(128)}, u32[]{:S(2)}) copy-start(f32[2]{0:T(128)} %param.21) | copy-start | bytes 28
  125.5 0.7 copy-start.2
Sparse Core Ops, SparseCore 0:
  9.6 34.9 all-gather.4
  46.4 27.1 all-gather.6
